TPU v7x, 32 devices: a whole 2x2x4 slice. The times are simulated.
32 devices in a mesh: tmpl: 4 (over y, core), seq: 2 (over x), tp: 4 (over z).
Axes of the slice: x: 2, y: 2, z: 4, core: 2. Of those that a mesh axis runs over, the one named last changes fastest.
Arguments:
- tokens: bfloat16 [3072, 5376], P(('tmpl', 'seq', 'tp')), parts along dimension 0, may hold values from -6 to 6
- lengths: int32 [8], P('tmpl'), parts along dimension 0, may hold values from 1 to 384, as said below
- input_gain: float32 [5376], replicated, may hold values from 0.1 to 1.9
- query_proj: bfloat16 [5376, 512], P(None, 'tp'), may hold values from -0.078125 to 0.078125
- key_value: bfloat16 [5376, 1024], P(None, 'tp'), may hold values from -0.078125 to 0.078125
- query_gain: float32 [128], replicated, may hold values from 0.5 to 20, as said below
- key_gain: float32 [128], replicated, may hold values from 0.5 to 6, as said below
- window_cache: bfloat16 [4096, 1024], P(('tmpl', 'seq'), 'tp'), parts along dimension 0, may hold values from -6 to 6
- output_proj: bfloat16 [512, 5376], P('tp', 'seq'), may hold values from -0.25 to 0.25
- post_gain: float32 [5376], replicated, may hold values from 0.1 to 1.9
Outputs:
- layer_out: bfloat16 [3072, 5376], P(('tmpl', 'seq', 'tp')), parts along dimension 0
There are 4 independent parts, one for each index of `tmpl`. A program takes and returns all parts, laid end to end along the dimension named above; an argument that names none is the same for every part. Nothing has to cross between parts.
Inputs may be any that keep to these rules, and one draw needn't show every extreme that they name: The template's live slab tokens fill the first lengths[s] slots of seq index s, in order of s; one entry equals 384. `query_gain`: positive entries. `key_gain`: positive entries.
All inputs are finite; a program needn't handle non-finite values.
Results may differ from a plain program's by a relative error of at most 0.018.
The roundings to bfloat16 on the way count: a program that leaves them out, or rounds other values in their place, can miss the bound.
Values may be sent and summed in bfloat16 or wider, within the bound.
A program may use at most 64 MiB of HBM per device.

v0:
```python
import jax
import jax.numpy as jnp
from jax import lax
from jax.sharding import PartitionSpec as P

WIN = 1024
PREFIX = 32768
EPSILON = 1e-06
ROPE_BASE = 10000.0
QUERY_SCALE = 168.0 ** (-0.5)
MASKED = -1e30


def normalize(values, scale_gain):
    values = values.astype(jnp.float32)
    return (
        values * lax.rsqrt(jnp.mean(values * values, axis=-1, keepdims=True) + EPSILON) * scale_gain
    )


def rotate(values, positions):
    half_width = values.shape[-1] // 2
    frequency = jnp.power(
        ROPE_BASE, -2.0 * jnp.arange(half_width, dtype=jnp.float32) / values.shape[-1]
    )
    angles = positions.astype(jnp.float32)[:, None] * frequency[None, :]
    cosine_table = jnp.cos(angles)
    sine_table = jnp.sin(angles)
    first_half = values[:, :half_width]
    second_half = values[:, half_width:]
    return jnp.concatenate(
        [
            first_half * cosine_table - second_half * sine_table,
            second_half * cosine_table + first_half * sine_table,
        ],
        axis=1,
    )


def shards(
    tokens,
    lengths,
    input_gain,
    query_proj,
    key_value,
    query_gain,
    key_gain,
    window_cache,
    output_proj,
    post_gain,
):
    row_count = tokens.shape[0]
    slab_slots = row_count * lax.axis_size("tp")
    head_width = query_proj.shape[1]
    cache_slots = window_cache.shape[0]
    block_rows = slab_slots + cache_slots
    shard_count = lengths.shape[0]
    shard_index = lax.axis_index("seq")
    normed = normalize(tokens, input_gain).astype(jnp.bfloat16)
    piece = lax.all_gather(normed, "tp", axis=0, tiled=True)
    projected = jnp.concatenate(
        [
            jnp.dot(piece, query_proj, preferred_element_type=jnp.float32),
            jnp.dot(piece, key_value, preferred_element_type=jnp.float32),
        ],
        axis=1,
    )
    offsets = jnp.cumsum(lengths) - lengths
    shard_ids = jnp.arange(shard_count, dtype=jnp.int32)
    own_length = jnp.sum(jnp.where(shard_ids == shard_index, lengths, 0))
    own_offset = jnp.sum(jnp.where(shard_ids == shard_index, offsets, 0))
    slot_index = jnp.arange(slab_slots, dtype=jnp.int32)
    positions = PREFIX + own_offset + slot_index
    live_rows = slot_index < own_length
    queries = (
        rotate(normalize(projected[:, :head_width], query_gain), positions) * QUERY_SCALE
    ).astype(jnp.bfloat16)
    new_keys = rotate(
        normalize(projected[:, head_width : 2 * head_width], key_gain), positions
    ).astype(jnp.bfloat16)
    new_values = projected[:, 2 * head_width :].astype(jnp.bfloat16)
    own_block = jnp.concatenate(
        [jnp.concatenate([new_keys, new_values], axis=1), window_cache], axis=0
    )
    gathered = lax.all_gather(own_block, "seq", axis=0, tiled=True)
    running_max = jnp.full((slab_slots,), MASKED, jnp.float32)
    key_rows = gathered[:, :head_width]
    value_rows = gathered[:, head_width:]
    key_index = 0 + jnp.arange(gathered.shape[0], dtype=jnp.int32)
    key_shard = key_index // block_rows
    inner_row = key_index % block_rows
    picked = key_shard[:, None] == shard_ids[None, :]
    shard_offset = jnp.sum(jnp.where(picked, offsets[None, :], 0), axis=1)
    shard_length = jnp.sum(jnp.where(picked, lengths[None, :], 0), axis=1)
    in_slab = inner_row < slab_slots
    key_position = jnp.where(
        in_slab,
        PREFIX + shard_offset + inner_row,
        PREFIX - WIN + key_shard * cache_slots + inner_row - slab_slots,
    )
    key_live = jnp.where(in_slab, inner_row < shard_length, True)
    key_position, key_live = (key_position, key_live)
    visible = (
        key_live[None, :]
        & (key_position[None, :] <= positions[:, None])
        & (key_position[None, :] > positions[:, None] - WIN)
    )
    scores = lax.dot_general(
        queries, key_rows, (((1,), (1,)), ((), ())), preferred_element_type=jnp.float32
    )
    scores = jnp.where(visible, scores, MASKED)
    new_max = jnp.maximum(running_max, jnp.max(scores, axis=1))
    weights = jnp.where(visible, jnp.exp(scores - new_max[:, None]), 0.0)
    running_sum = jnp.sum(weights, axis=1)
    running_acc = jnp.dot(
        weights.astype(jnp.bfloat16), value_rows, preferred_element_type=jnp.float32
    )
    head_out = running_acc / jnp.where(live_rows, running_sum, 1.0)[:, None]
    head_out = jnp.where(live_rows[:, None], head_out, 0.0).astype(jnp.bfloat16)
    full_weights = lax.all_gather(output_proj, "seq", axis=1, tiled=True)
    projection = lax.psum_scatter(
        jnp.dot(head_out, full_weights, preferred_element_type=jnp.float32).astype(jnp.bfloat16),
        "tp",
        scatter_dimension=0,
        tiled=True,
    ).astype(jnp.float32)
    post_norm = normalize(projection, post_gain)
    return (tokens.astype(jnp.float32) + post_norm).astype(jnp.bfloat16)


def solution(mesh):
    return jax.shard_map(
        shards,
        mesh=mesh,
        in_specs=(
            P(("tmpl", "seq", "tp"), None),
            P("tmpl"),
            P(),
            P(None, "tp"),
            P(None, "tp"),
            P(),
            P(),
            P(("tmpl", "seq"), "tp"),
            P("tp", "seq"),
            P(),
        ),
        out_specs=P(("tmpl", "seq", "tp"), None),
        check_vma=False,
    )
```

profile of v0, /device:TPU:0, one launch (start us, length us, event | category | flops | bytes accessed | tf_op | source)
XLA Modules:
  0.0 221.9 jit_solution(13530554699072405083)
XLA Ops:
  6.5 0.0 copy-start
  6.5 0.0 copy-start.7
  6.5 0.0 all-gather.3.cloned.1.call-start
  6.5 1.7 fusion.2
  8.2 2.5 %fusion.4 = bf16[96,5376]{1,0:T(8,128)(2,1)} fusion(bf16[96,5376]{1,0:T(8,128)(2,1)} %param.10, f32[5376]{0:T(1024)} %param.12, f32[96]{0:T(128)S(1)} %add_rsqrt_fusion.3), kind=kLoop, calls=%fused_computation.13 | loop fusion | flops 2064384 | bytes 2086272 | tf_op jit(solution)/shard_map/convert_element_type | solution.py:59
  10.7 0.0 all-gather.3.cloned.1.call-update
  10.8 0.0 all-gather.5.cloned.1.call-start
  10.8 0.7 all-gather.5.cloned.1.call-update
  11.5 0.0 reduce-scatter.2.cloned.1.call-start
  11.6 0.0 copy-done.7
  11.6 0.2 reduce-window.9
  11.8 0.7 fusion.57
  13.2 0.6 iota_compare_fusion.1
  13.8 0.1 select_reduce_fusion.1
  14.0 79.3 %all-gather.3.cloned.1.call-done = bf16[384,5376]{1,0:T(8,128)(2,1)} async-done(((bf16[96,5376]{1,0:T(8,128)(2,1)}), bf16[384,5376]{1,0:T(8,128)(2,1)}) %all-gather.3.cloned.1.call-update) | async-done | bytes 4128784 | tf_op jit(solution)/shard_map/all_gather | solution.py:60
  93.3 0.0 copy-done
  93.3 0.0 copy-start.1
  93.3 0.0 copy-start.3
  93.3 4.0 %fusion.63 = f32[384,256]{0,1:T(8,128)S(1)} fusion(bf16[384,5376]{1,0:T(8,128)(2,1)} %all-gather.3.cloned.1.call-done, bf16[5376,256]{1,0:T(8,128)(2,1)S(1)} %copy-done), kind=kOutput, calls=%fused_computation.91 | convolution fusion | flops 1056964608 | bytes 7274496 | tf_op jit(solution)/shard_map/dot_general | solution.py:64
  97.3 0.0 copy-done.1
  97.3 0.0 copy-done.3
  97.3 0.0 copy-start.8
  97.3 0.0 copy-start.9
  97.4 0.0 copy-start.5
  97.4 1.3 multiply_reduce_fusion.1
  98.7 0.0 copy-done.8
  98.7 0.0 copy-done.9
  98.7 0.1 multiply_multiply_fusion
  98.8 1.1 fusion.35
  100.0 0.1 copy.12
  100.1 0.0 copy-done.5
  100.2 23.1 %all_gather.10 = bf16[1792,256]{1,0:T(8,128)(2,1)S(1)} all-gather(bf16[896,256]{1,0:T(8,128)(2,1)S(1)} %pad_maximum_fusion), channel_id=1, replica_groups=mesh['tmpl'=4,'seq'=2,'tp'=4] {'seq'}, dimensions={0}, use_global_device_ids=true | all-gather | bytes 1376256 | tf_op jit(solution)/shard_map/all_gather | solution.py:85
  123.3 0.0 copy-start.4
  123.3 0.9 copy-done.4
  124.2 2.0 fusion.62
  126.3 0.0 copy-start.2
  126.3 1.5 copy-done.2
  127.8 1.2 fusion.6
  129.0 0.6 broadcast_select_fusion
  129.7 0.0 all-gather.5.cloned.1.call-done
  129.7 6.9 %convolution_convert_fusion = bf16[384,5376]{1,0:T(8,128)(2,1)} fusion(bf16[128,5376]{1,0:T(8,128)(2,1)} %all-gather.5.cloned.1.call-done, f32[384,1792]{1,0:T(8,128)} %copy-done.2, f32[384]{0:T(512)S(1)} %broadcast_maximum_fusion, bf16[1792,256]{1,0:T(8,128)(2,1)} %copy-done.4, f32[384]{0:T(512)S(1)} %broadcast_select_fusion, ...), kind=kOutput, calls=%fused_computation | convolution fusion | flops 711671808 | bytes 8731776 | tf_op jit(solution)/shard_map/dot_general | solution.py:122
  136.6 0.0 copy-start.6
  136.6 0.0 reduce-scatter.2.cloned.1.call-update
  136.6 74.3 %reduce-scatter.2.cloned.1.call-done = bf16[96,5376]{1,0:T(8,128)(2,1)} async-done(((bf16[384,5376]{1,0:T(8,128)(2,1)}), bf16[96,5376]{1,0:T(8,128)(2,1)}) %reduce-scatter.2.cloned.1.call-update) | async-done | bytes 1032208 | tf_op jit(solution)/shard_map/reduce_scatter | solution.py:121
  210.9 1.5 fusion
  212.4 0.0 copy-done.6
  212.4 2.9 %fusion.5 = bf16[96,5376]{1,0:T(8,128)(2,1)} fusion(bf16[96,5376]{1,0:T(8,128)(2,1)} %reduce-scatter.2.cloned.1.call-done, bf16[96,5376]{1,0:T(8,128)(2,1)} %param.10, f32[5376]{0:T(1024)S(1)} %copy-done.6, f32[96]{0:T(128)S(1)} %add_rsqrt_fusion.2), kind=kLoop, calls=%fused_computation.14 | loop fusion | flops 3096576 | bytes 3118464 | tf_op jit(solution)/shard_map/convert_element_type | solution.py:128
  (15 shorter events, 0.2 us)
Async XLA Ops:
  6.5 86.8 %copy-start = (bf16[5376,256]{1,0:T(8,128)(2,1)S(1)}, bf16[5376,256]{1,0:T(8,128)(2,1)}, u32[]{:S(2)}) copy-start(bf16[5376,256]{1,0:T(8,128)(2,1)} %param.14) | copy-start | bytes 8257540
  6.5 5.0 %copy-start.7 = (s32[2]{0:T(128)S(1)}, s32[2]{0:T(128)}, u32[]{:S(2)}) copy-start(s32[2]{0:T(128)} %param.11) | copy-start | bytes 28
  6.5 86.8 %all-gather.3.cloned.1.call-start = ((), (), s32[]{:S(2)}) async-start(), calls=%async_computation.1 | async-start | bytes 5160960 | tf_op jit(solution)/shard_map/all_gather | solution.py:60
  10.8 118.9 %all-gather.5.cloned.1.call-start = ((), (), s32[]{:S(2)}) async-start(), calls=%async_computation.2 | async-start | bytes 2064384 | tf_op jit(solution)/shard_map/all_gather | solution.py:120
  11.5 199.4 %reduce-scatter.2.cloned.1.call-start = ((), (), s32[]{:S(2)}) async-start(), calls=%async_computation.3 | async-start | bytes 5160960 | tf_op jit(solution)/shard_map/reduce_scatter | solution.py:121
  93.3 4.0 %copy-start.1 = (bf16[384,5376]{1,0:T(8,128)(2,1)S(1)}, bf16[384,5376]{1,0:T(8,128)(2,1)}, u32[]{:S(2)}) copy-start(bf16[384,5376]{1,0:T(8,128)(2,1)} %all-gather.3.cloned.1.call-done) | copy-start | bytes 12386308
  93.3 4.0 %copy-start.3 = (bf16[5376,128]{1,0:T(8,128)(2,1)S(1)}, bf16[5376,128]{1,0:T(8,128)(2,1)}, u32[]{:S(2)}) copy-start(bf16[5376,128]{1,0:T(8,128)(2,1)} %param.13) | copy-start | bytes 4128772
  97.3 1.4 copy-start.8
  97.3 1.4 copy-start.9
  97.4 2.8 %copy-start.5 = (bf16[512,256]{1,0:T(8,128)(2,1)S(1)}, bf16[512,256]{1,0:T(8,128)(2,1)}, u32[]{:S(2)}) copy-start(bf16[512,256]{1,0:T(8,128)(2,1)} %param.17) | copy-start | bytes 786436
  123.3 0.9 copy-start.4
  126.3 1.5 copy-start.2
  136.6 75.8 %copy-start.6 = (f32[5376]{0:T(1024)S(1)}, f32[5376]{0:T(1024)}, u32[]{:S(2)}) copy-start(f32[5376]{0:T(1024)} %param.19) | copy-start | bytes 64516
Sparse Core Ops, SparseCore 0:
  10.9 82.3 all-gather.2
  94.8 33.0 all-gather.4
  136.7 74.1 reduce-scatter.1
where the time goes:
time: 222 us
  waiting for transfers between devices  154 us (69%)
  blocking collectives  23.1 us (10%)
  matrix products  14.2 us (6%)
  between operations  14 us (6%)
  other arithmetic  13.5 us (6%)
  local copies, waits for them, and re-layouts  2.63 us (1%)
    all_gather x1, waiting for transfers between devices, shards(): piece = lax.all_gather(normed, 'tp', axis=0, tiled=True)  79.3 us
    reduce_scatter x1, waiting for transfers between devices, shards(): lax.psum_scatter(jnp.dot(head_out, full_weights, preferred_element_type=j...  74.3 us
    all_gather x1, blocking collectives, shards(): gathered = lax.all_gather(own_block, 'seq', axis=0, tiled=True)  23.1 us
    dot_general x1, matrix products, shards(): jnp.dot(head_out, full_weights, preferred_element_type=jnp.float32)  6.89 us
  transfers between devices with their start and end apart: 3, of which 2 were waited for; matrix products, arithmetic and copies ran while one was open for 6% of the time, Pallas kernels for 0%

commit v1 on v0

--- a/solution.py
+++ b/solution.py
@@ -57,7 +57,23 @@
     shard_count = lengths.shape[0]
     shard_index = lax.axis_index("seq")
     normed = normalize(tokens, input_gain).astype(jnp.bfloat16)
-    piece = lax.all_gather(normed, "tp", axis=0, tiled=True)
+
+    def _bring_entries(unit):
+        inbox = [unit]
+        cores_n = lax.psum(1, axis_name="tp")
+        for q in tuple(range(cores_n - 1)):
+            inbox.append(
+                lax.ppermute(
+                    inbox[-1], axis_name="tp", perm=[(k, (k + 1) % cores_n) for k in range(cores_n)]
+                )
+            )
+        return jnp.roll(
+            jnp.concatenate(inbox[::-1], axis=0),
+            shift=(lax.axis_index("tp") + 1) * unit.shape[0],
+            axis=0,
+        )
+
+    piece = _bring_entries(normed)
     projected = jnp.concatenate(
         [
             jnp.dot(piece, query_proj, preferred_element_type=jnp.float32),

time: 222 us -> 212 us (0.955)
  blocking collectives: 23.1 us -> 10.8 us
  local copies, waits for them, and re-layouts: 2.63 us -> 10.4 us
  waiting for transfers between devices: 154 us -> 147 us
  starting transfers between devices: 0.08 us -> 3.15 us
    all_gather x1 -> x0, waiting for transfers between devices: 79.3 us -> none  [shards(): piece = lax.all_gather(normed, 'tp', axis=0, tiled=True)]
    ppermute x0 -> x3, waiting for transfers between devices: none -> 73.7 us  [_bring_entries(): lax.ppermute(inbox[-1], axis_name='tp', perm=[(k, (k + 1) % cores_n) for...]
    all_gather x1, blocking collectives: 23.1 us -> 10.8 us  [shards(): gathered = lax.all_gather(own_block, 'seq', axis=0, tiled=True)]
    unnamed x20 -> x28, local copies, waits for them, and re-layouts: 2.47 us -> 10.3 us
    ppermute x0 -> x3, starting transfers between devices: none -> 3.11 us  [_bring_entries(): lax.ppermute(inbox[-1], axis_name='tp', perm=[(k, (k + 1) % cores_n) for...]
    dot_general x1, matrix products: 3.95 us -> 1.69 us  [shards(): jnp.dot(piece, key_value, preferred_element_type=jnp.float32)]
  transfers between devices with their start and end apart: 3 -> 5, of which waited for: 2 -> 4; matrix products, arithmetic and copies ran while one was open for 6% -> 9% of each run, Pallas kernels for 0% -> 0%
where the time goes in v1:
time: 212 us; the launch traced here: 211 us
  waiting for transfers between devices  147 us (69%)
  between operations  14.4 us (7%)
  other arithmetic  13.2 us (6%)
  matrix products  12.1 us (6%)
  blocking collectives  10.8 us (5%)
  local copies, waits for them, and re-layouts  10.4 us (5%)
  starting transfers between devices  3.15 us (1%)
    ppermute x3, waiting for transfers between devices, _bring_entries(): lax.ppermute(inbox[-1], axis_name='tp', perm=[(k, (k + 1) % cores_n) for...  73.7 us
    reduce_scatter x1, waiting for transfers between devices, shards(): lax.psum_scatter(jnp.dot(head_out, full_weights, preferred_element_type=j...  73.4 us
    all_gather x1, blocking collectives, shards(): gathered = lax.all_gather(own_block, 'seq', axis=0, tiled=True)  10.8 us
    unnamed x28, local copies, waits for them, and re-layouts  10.3 us
    dot_general x1, matrix products, shards(): jnp.dot(head_out, full_weights, preferred_element_type=jnp.float32)  6.84 us
  transfers between devices with their start and end apart: 5, of which 4 were waited for; matrix products, arithmetic and copies ran while one was open for 9% of the time, Pallas kernels for 0%

profile of v1, /device:TPU:0, one launch (start us, length us, event | category | flops | bytes accessed | tf_op | source)
XLA Modules:
  0.0 211.2 jit_solution(3976678394375951777)
XLA Ops:
  6.5 1.7 fusion.6
  8.2 1.5 fusion.8
  9.8 3.1 %collective-permute-start = (bf16[96,5376]{1,0:T(8,128)(2,1)S(1)}, bf16[96,5376]{1,0:T(8,128)(2,1)}, u32[]{:S(2)}, u32[]{:S(2)}) collective-permute-start(bf16[96,5376]{1,0:T(8,128)(2,1)S(1)} %fusion.8), channel_id=1, source_target_pairs={{0,1},{1,2},{2,3},{3,0},{4,5},{5,6},{6,7},{7,4},{8,9},{9,10},{10,1... | collective-permute-start | bytes 3096584 | tf_op jit(solution)/shard_map/ppermute | solution.py:66
  12.9 24.9 %collective-permute-done = bf16[96,5376]{1,0:T(8,128)(2,1)} collective-permute-done((bf16[96,5376]{1,0:T(8,128)(2,1)S(1)}, bf16[96,5376]{1,0:T(8,128)(2,1)}, u32[]{:S(2)}, u32[]{:S(2)}) %collective-permute-start) | collective-permute-done | bytes 1032224 | tf_op jit(solution)/shard_map/ppermute | solution.py:66
  37.8 0.0 collective-permute-start.1
  37.8 0.0 all-gather.2.cloned.1.call-update
  37.8 0.0 reduce-scatter.2.cloned.1.call-start
  37.9 0.2 reduce-window.9
  38.1 0.7 fusion.61
  38.8 25.1 %collective-permute-done.1 = bf16[96,5376]{1,0:T(8,128)(2,1)} collective-permute-done((bf16[96,5376]{1,0:T(8,128)(2,1)}, bf16[96,5376]{1,0:T(8,128)(2,1)}, u32[]{:S(2)}, u32[]{:S(2)}) %collective-permute-start.1) | collective-permute-done | bytes 1032224 | tf_op jit(solution)/shard_map/ppermute | solution.py:66
  63.9 0.0 collective-permute-start.2
  64.6 0.7 iota_compare_fusion.1
  65.3 0.1 select_reduce_fusion.1
  65.5 0.0 copy-start.1
  65.5 0.0 copy-start.5
  65.5 23.6 %collective-permute-done.2 = bf16[96,5376]{1,0:T(8,128)(2,1)} collective-permute-done((bf16[96,5376]{1,0:T(8,128)(2,1)}, bf16[96,5376]{1,0:T(8,128)(2,1)}, u32[]{:S(2)}, u32[]{:S(2)}) %collective-permute-start.2) | collective-permute-done | bytes 1032224 | tf_op jit(solution)/shard_map/ppermute | solution.py:66
  89.1 1.3 constant_dynamic-update-slice_fusion.7
  90.4 1.3 constant_dynamic-update-slice_fusion.6
  91.7 1.3 constant_dynamic-update-slice_fusion.5
  93.0 0.0 copy-done.1
  93.0 0.0 copy-done.5
  93.0 0.3 constant_dynamic-update-slice_fusion.4
  93.3 1.3 constant_dynamic-update-slice_fusion.3
  94.6 1.3 constant_dynamic-update-slice_fusion.2
  95.9 1.3 constant_dynamic-update-slice_fusion.1
  97.2 0.3 constant_dynamic-update-slice_fusion
  97.5 0.0 copy-done
  97.5 0.0 copy-start.10
  97.5 1.7 fusion
  99.3 0.0 copy-start.8
  99.3 0.0 copy-start.9
  99.3 0.0 copy-start.4
  99.4 1.5 multiply_reduce_fusion.1
  100.9 0.1 multiply_multiply_fusion
  101.0 1.1 fusion.39
  102.1 0.1 copy.12
  102.3 10.8 %all_gather.6 = bf16[1792,256]{1,0:T(8,128)(2,1)S(1)} all-gather(bf16[896,256]{1,0:T(8,128)(2,1)S(1)} %pad_maximum_fusion), channel_id=1, replica_groups=mesh['tmpl'=4,'seq'=2,'tp'=4] {'seq'}, dimensions={0}, use_global_device_ids=true | all-gather | bytes 1376256 | tf_op jit(solution)/shard_map/all_gather | solution.py:101
  113.1 0.9 copy-done.3
  114.1 2.0 fusion.68
  116.1 1.6 copy-done.2
  117.7 1.2 fusion.10
  118.9 0.7 broadcast_select_fusion
  119.6 0.0 all-gather.2.cloned.1.call-done
  119.6 6.8 %convolution_convert_fusion = bf16[384,5376]{1,0:T(8,128)(2,1)} fusion(bf16[128,5376]{1,0:T(8,128)(2,1)} %all-gather.2.cloned.1.call-done, f32[384,1792]{1,0:T(8,128)} %copy-done.2, f32[384]{0:T(512)S(1)} %broadcast_maximum_fusion, bf16[1792,256]{1,0:T(8,128)(2,1)} %copy-done.3, f32[384]{0:T(512)S(1)} %broadcast_select_fusion, ...), kind=kOutput, calls=%fused_computation | convolution fusion | flops 711671808 | bytes 8731776 | tf_op jit(solution)/shard_map/dot_general | solution.py:138
  126.5 0.0 reduce-scatter.2.cloned.1.call-update
  126.5 73.4 %reduce-scatter.2.cloned.1.call-done = bf16[96,5376]{1,0:T(8,128)(2,1)} async-done(((bf16[384,5376]{1,0:T(8,128)(2,1)}), bf16[96,5376]{1,0:T(8,128)(2,1)}) %reduce-scatter.2.cloned.1.call-update) | async-done | bytes 1032208 | tf_op jit(solution)/shard_map/reduce_scatter | solution.py:137
  199.9 1.5 fusion.4
  201.5 2.9 %fusion.9 = bf16[96,5376]{1,0:T(8,128)(2,1)} fusion(bf16[96,5376]{1,0:T(8,128)(2,1)} %reduce-scatter.2.cloned.1.call-done, bf16[96,5376]{1,0:T(8,128)(2,1)} %param.10, f32[5376]{0:T(1024)S(1)} %copy-done.6, f32[96]{0:T(128)S(1)} %add_rsqrt_fusion.2), kind=kLoop, calls=%fused_computation.18 | loop fusion | flops 3096576 | bytes 3118464 | tf_op jit(solution)/shard_map/convert_element_type | solution.py:144
  (27 shorter events, 0.2 us)
Async XLA Ops:
  6.5 91.0 %copy-start = (bf16[5376,256]{1,0:T(8,128)(2,1)S(1)}, bf16[5376,256]{1,0:T(8,128)(2,1)}, u32[]{:S(2)}) copy-start(bf16[5376,256]{1,0:T(8,128)(2,1)} %param.14) | copy-start | bytes 8257540
  6.5 31.4 %copy-start.7 = (s32[2]{0:T(128)S(1)}, s32[2]{0:T(128)}, u32[]{:S(2)}) copy-start(s32[2]{0:T(128)} %param.11) | copy-start | bytes 28
  6.5 113.1 %all-gather.2.cloned.1.call-start = ((), (), s32[]{:S(2)}) async-start(), calls=%async_computation.1 | async-start | bytes 2064384 | tf_op jit(solution)/shard_map/all_gather | solution.py:136
  9.8 28.0 %collective-permute-start = (bf16[96,5376]{1,0:T(8,128)(2,1)S(1)}, bf16[96,5376]{1,0:T(8,128)(2,1)}, u32[]{:S(2)}, u32[]{:S(2)}) collective-permute-start(bf16[96,5376]{1,0:T(8,128)(2,1)S(1)} %fusion.8), channel_id=1, source_target_pairs={{0,1},{1,2},{2,3},{3,0},{4,5},{5,6},{6,7},{7,4},{8,9},{9,10},{10,1... | collective-permute-start | bytes 3096584 | tf_op jit(solution)/shard_map/ppermute | solution.py:66
  37.8 26.1 %collective-permute-start.1 = (bf16[96,5376]{1,0:T(8,128)(2,1)}, bf16[96,5376]{1,0:T(8,128)(2,1)}, u32[]{:S(2)}, u32[]{:S(2)}) collective-permute-start(bf16[96,5376]{1,0:T(8,128)(2,1)} %collective-permute-done), channel_id=1, source_target_pairs={{0,1},{1,2},{2,3},{3,0},{4,5},{5,6},{6,7},{7,4},{8,9},{9,10},{10,1... | collective-permute-start | bytes 3096584 | tf_op jit(solution)/shard_map/ppermute | solution.py:66
  37.8 162.1 %reduce-scatter.2.cloned.1.call-start = ((), (), s32[]{:S(2)}) async-start(), calls=%async_computation.2 | async-start | bytes 5160960 | tf_op jit(solution)/shard_map/reduce_scatter | solution.py:137
  63.9 25.2 %collective-permute-start.2 = (bf16[96,5376]{1,0:T(8,128)(2,1)}, bf16[96,5376]{1,0:T(8,128)(2,1)}, u32[]{:S(2)}, u32[]{:S(2)}) collective-permute-start(bf16[96,5376]{1,0:T(8,128)(2,1)} %collective-permute-done.1), channel_id=1, source_target_pairs={{0,1},{1,2},{2,3},{3,0},{4,5},{5,6},{6,7},{7,4},{8,9},{9,10},{10,1... | collective-permute-start | bytes 3096584 | tf_op jit(solution)/shard_map/ppermute | solution.py:66
  65.5 27.5 %copy-start.1 = (bf16[96,5376]{1,0:T(8,128)(2,1)S(1)}, bf16[96,5376]{1,0:T(8,128)(2,1)}, u32[]{:S(2)}) copy-start(bf16[96,5376]{1,0:T(8,128)(2,1)} %param.10) | copy-start | bytes 3096580
  65.5 27.5 %copy-start.5 = (f32[5376]{0:T(1024)S(1)}, f32[5376]{0:T(1024)}, u32[]{:S(2)}) copy-start(f32[5376]{0:T(1024)} %param.12) | copy-start | bytes 64516
  97.5 1.8 copy-start.10
  99.3 1.6 copy-start.8
  99.3 1.6 copy-start.9
  99.3 2.9 %copy-start.4 = (bf16[512,256]{1,0:T(8,128)(2,1)S(1)}, bf16[512,256]{1,0:T(8,128)(2,1)}, u32[]{:S(2)}) copy-start(bf16[512,256]{1,0:T(8,128)(2,1)} %param.17) | copy-start | bytes 786436
  113.1 0.9 copy-start.3
  116.1 1.6 copy-start.2
  126.5 75.0 %copy-start.6 = (f32[5376]{0:T(1024)S(1)}, f32[5376]{0:T(1024)}, u32[]{:S(2)}) copy-start(f32[5376]{0:T(1024)} %param.19) | copy-start | bytes 64516
Sparse Core Ops, SparseCore 0:
  38.0 26.4 all-gather.1
  126.6 73.2 reduce-scatter.1
